TPU v7x, 32 devices: a whole 2x2x4 slice. The times are simulated.
32 devices in a mesh: ctx: 2 (over x), dp: 4 (over z), tp: 4 (over y, core).
Axes of the slice: x: 2, y: 2, z: 4, core: 2. Of those that a mesh axis runs over, the one named last changes fastest.
Arguments:
- query_act: bfloat16 [4, 4096, 256], P('dp', 'tp', 'ctx'), may hold values from -6 to 6
- key_act: bfloat16 [4, 4096, 256], P('dp', 'tp', 'ctx'), may hold values from -6 to 6
- value_act: bfloat16 [4, 4096, 256], P('dp', 'tp', 'ctx'), may hold values from -6 to 6
- out_grad: bfloat16 [4, 4096, 256], P('dp', 'tp', 'ctx'), may hold values from -6 to 6
- keep_mask: int32 [4, 256], P('dp', 'ctx'), may hold values 0 or 1
- filter_taps: float32 [256, 128], P('tp'), may hold values from -0.5 to 0.5
- skip_gain: float32 [4096], P('tp'), may hold values from -4 to 4
Outputs:
- operator_out: bfloat16 [4, 4096, 256], P('dp', 'tp', 'ctx')
- query_grad: bfloat16 [4, 4096, 256], P('dp', 'tp', 'ctx')
- key_grad: bfloat16 [4, 4096, 256], P('dp', 'tp', 'ctx')
- value_grad: bfloat16 [4, 4096, 256], P('dp', 'tp', 'ctx')
- filter_grad: float32 [256, 128], P('tp')
- skip_grad: float32 [4096], P('tp')
All inputs are finite; a program needn't handle non-finite values. No bound on the sum of `keep_mask` on one device may be relied on, other than what follows from the above.
Results may differ from a plain program's by a relative error of at most 0.007.
Values may be sent and summed in bfloat16 or wider, within the bound.
No kernel may reach another device: no remote copies, remote signals or barrier semaphores. Data moves between devices by JAX's collectives and lax.ppermute only.
A program may use at most 64 MiB of HBM per device.

v0:
```python
import math
import jax
import jax.numpy as jnp
from jax import lax
from jax.sharding import PartitionSpec as P


def tap_matrices(tap_rows):
    tap_len = tap_rows.shape[1]
    source = jnp.arange(tap_len)[:, None]
    target = jnp.arange(tap_len)[None, :]
    spread = tap_rows[:, jnp.mod(target - source, tap_len)]
    nothing = jnp.zeros((), jnp.bfloat16)
    lower_part = jnp.where(target >= source, spread, nothing)
    upper_part = jnp.where(target < source, spread, nothing)
    forward = jnp.concatenate([upper_part, lower_part], axis=1)
    backward = jnp.concatenate(
        [jnp.swapaxes(lower_part, 1, 2), jnp.swapaxes(upper_part, 1, 2)], axis=1
    )
    return (forward, backward)


def diagonal_sums(gram_sums):
    groups, tap_len, double_len = gram_sums.shape
    flattened = gram_sums.reshape(groups, tap_len * double_len)
    flattened = jnp.pad(flattened, ((0, 0), (0, tap_len)))
    skewed = flattened.reshape(groups, tap_len, double_len + 1)
    columns = jnp.sum(skewed, axis=1)
    return columns[:, tap_len:0:-1]


def core(
    query_act, key_act, value_act, scaled_grad, filter_taps, skip_gain, fetch_left, fetch_right
):
    windows, channels, length = query_act.shape
    groups, tap_len = filter_taps.shape
    per_group = channels // groups
    blocks = length // tap_len
    forward, backward = tap_matrices(filter_taps.astype(jnp.bfloat16))
    joined = (key_act.astype(jnp.float32) * value_act.astype(jnp.float32)).astype(jnp.bfloat16)
    before = fetch_left(joined[:, :, length - tap_len :])
    joined_blocks = joined.reshape(windows, channels, blocks, tap_len)
    earlier = jnp.concatenate([before[:, :, None, :], joined_blocks[:, :, :-1, :]], axis=2)
    paired = jnp.concatenate([earlier, joined_blocks], axis=3).reshape(
        windows, groups, per_group, blocks, 2 * tap_len
    )
    mixed_sum = jnp.einsum("wgcbs,gst->wgcbt", paired, forward, preferred_element_type=jnp.float32)
    mixed_sum = mixed_sum.reshape(windows, channels, length) + skip_gain[
        None, :, None
    ] * joined.astype(jnp.float32)
    operator_out = (query_act.astype(jnp.float32) * mixed_sum).astype(jnp.bfloat16)
    mixed_grad = (scaled_grad.astype(jnp.float32) * query_act.astype(jnp.float32)).astype(
        jnp.bfloat16
    )
    query_grad = (scaled_grad.astype(jnp.float32) * mixed_sum).astype(jnp.bfloat16)
    following = fetch_right(mixed_grad[:, :, :tap_len])
    grad_blocks = mixed_grad.reshape(windows, channels, blocks, tap_len)
    next_blocks = jnp.concatenate([grad_blocks[:, :, 1:, :], following[:, :, None, :]], axis=2)
    paired_grad = jnp.concatenate([grad_blocks, next_blocks], axis=3).reshape(
        windows, groups, per_group, blocks, 2 * tap_len
    )
    joined_grad = jnp.einsum(
        "wgcbs,gst->wgcbt", paired_grad, backward, preferred_element_type=jnp.float32
    )
    joined_grad = joined_grad.reshape(windows, channels, length) + skip_gain[
        None, :, None
    ] * mixed_grad.astype(jnp.float32)
    key_grad = (joined_grad * value_act.astype(jnp.float32)).astype(jnp.bfloat16)
    value_grad = (joined_grad * key_act.astype(jnp.float32)).astype(jnp.bfloat16)
    grad_groups = grad_blocks.reshape(windows, groups, per_group, blocks, tap_len)
    gram_sums = jnp.einsum(
        "wgcbt,wgcbs->gts", grad_groups, paired, preferred_element_type=jnp.float32
    )
    tap_sums = diagonal_sums(gram_sums)
    skip_sums = jnp.sum(mixed_grad.astype(jnp.float32) * joined.astype(jnp.float32), axis=(0, 2))
    return (operator_out, query_grad, key_grad, value_grad, tap_sums, skip_sums)


def no_rim(border):
    return jnp.zeros_like(border)


def body(query_act, key_act, value_act, out_grad, keep_mask, filter_taps, skip_gain):
    total_windows = keep_mask.shape[0] * lax.axis_size("dp")
    total_length = query_act.shape[2] * lax.axis_size("ctx")
    per_group = query_act.shape[1] // filter_taps.shape[0]
    tap_scale = 1.0 / math.sqrt(total_windows * total_length * per_group)
    skip_scale = 1.0 / math.sqrt(total_windows * total_length)
    scaled_grad = out_grad * keep_mask.astype(jnp.bfloat16)[:, None, :]
    moved = (
        lax.all_to_all(query_act, "ctx", split_axis=1, concat_axis=2, tiled=True),
        lax.all_to_all(key_act, "ctx", split_axis=1, concat_axis=2, tiled=True),
        lax.all_to_all(value_act, "ctx", split_axis=1, concat_axis=2, tiled=True),
        lax.all_to_all(scaled_grad, "ctx", split_axis=1, concat_axis=2, tiled=True),
    )
    shards = lax.axis_size("ctx")
    position = lax.axis_index("ctx")
    group_count = filter_taps.shape[0] // shards
    own_taps = lax.dynamic_slice_in_dim(filter_taps, position * group_count, group_count, 0)
    own_skip = lax.dynamic_slice_in_dim(
        skip_gain, position * group_count * per_group, group_count * per_group, 0
    )
    results = core(moved[0], moved[1], moved[2], moved[3], own_taps, own_skip, no_rim, no_rim)
    returned = (
        lax.all_to_all(results[0], "ctx", split_axis=2, concat_axis=1, tiled=True),
        lax.all_to_all(results[1], "ctx", split_axis=2, concat_axis=1, tiled=True),
        lax.all_to_all(results[2], "ctx", split_axis=2, concat_axis=1, tiled=True),
        lax.all_to_all(results[3], "ctx", split_axis=2, concat_axis=1, tiled=True),
    )
    replica = lax.psum((results[4], results[5]), "dp")
    gathered = (
        lax.all_gather(replica[0], "ctx", axis=0, tiled=True),
        lax.all_gather(replica[1], "ctx", axis=0, tiled=True),
    )
    tap_sums = gathered[0]
    skip_sums = gathered[1]
    return (
        returned[0],
        returned[1],
        returned[2],
        returned[3],
        tap_sums * tap_scale,
        skip_sums * skip_scale,
    )


def solution(mesh):
    return jax.shard_map(
        body,
        mesh=mesh,
        in_specs=(
            P("dp", "tp", "ctx"),
            P("dp", "tp", "ctx"),
            P("dp", "tp", "ctx"),
            P("dp", "tp", "ctx"),
            P("dp", "ctx"),
            P("tp", None),
            P("tp"),
        ),
        out_specs=(
            P("dp", "tp", "ctx"),
            P("dp", "tp", "ctx"),
            P("dp", "tp", "ctx"),
            P("dp", "tp", "ctx"),
            P("tp", None),
            P("tp"),
        ),
        check_vma=False,
    )
```

profile of v0, /device:TPU:0, one launch (start us, length us, event | category | flops | bytes accessed | tf_op | source)
XLA Modules:
  0.0 214.4 jit_solution(10341014407572912905)
XLA Ops:
  3.3 2.2 %reduce.3 = bf16[1024,128]{1,0:T(8,128)(2,1)S(1)} reduce(bf16[1024,1,128]{2,1,0:T(2,128)(2,1)S(1)} %fusion.30, bf16[]{:T(256)} %broadcast.146), dimensions={1}, to_apply=%fusion.30.reduce_sub_computation | reduce | bytes 524290
  6.3 4.2 %all-to-all-start.4 = ((bf16[2,2,32768]{2,1,0:T(2,128)(2,1)}), bf16[2,2,32768]{2,1,0:T(2,128)(2,1)S(1)}, u32[]{:S(2)}, u32[]{:S(2)}) async-start(bf16[2,2,32768]{2,1,0:T(2,128)(2,1)} %reshape.430), calls=%async_computation.4 | async-start | bytes 524288 | tf_op jit(solution)/shard_map/all_to_all | solution.py:94
  10.8 57.4 %gather_fusion = bf16[16384,32]{1,0:T(8,128)(2,1)} fusion(bf16[32,128]{0,1:T(8,128)(2,1)S(1)} %copy.92, s32[16384]{0:T(1024)S(1)} %fusion.22), kind=kCustom, calls=%fused_computation | custom fusion | bytes 2162688 | tf_op jit(solution)/shard_map/gather | solution.py:12
  68.2 4.0 %copy.82 = bf16[128,128,32]{1,0,2:T(8,128)(2,1)S(1)} copy(bf16[128,128,32]{2,1,0:T(8,128)(2,1)} %bitcast.156) | data formatting | bytes 2097152 | tf_op jit(solution)/shard_map/gather | solution.py:12
  75.5 2.2 %reduce.2 = bf16[1024,128]{1,0:T(8,128)(2,1)S(1)} reduce(bf16[1024,1,128]{2,1,0:T(2,128)(2,1)S(1)} %bitcast.187, bf16[]{:T(256)} %broadcast.146), dimensions={1}, to_apply=%bitcast.153.reduce_sub_computation | reduce | bytes 524290
  78.9 2.2 %reduce.4 = bf16[1024,128]{1,0:T(8,128)(2,1)S(1)} reduce(bf16[1024,1,128]{2,1,0:T(2,128)(2,1)S(1)} %bitcast.188, bf16[]{:T(256)} %broadcast.146), dimensions={1}, to_apply=%bitcast.152.reduce_sub_computation | reduce | bytes 524290
  82.3 2.2 %reduce.1 = bf16[1024,128]{1,0:T(8,128)(2,1)S(1)} reduce(bf16[1024,1,128]{2,1,0:T(2,128)(2,1)S(1)} %bitcast.189, bf16[]{:T(256)} %broadcast.146), dimensions={1}, to_apply=%bitcast.151.reduce_sub_computation | reduce | bytes 524290
  85.4 3.5 %all-to-all-start = ((bf16[2,2,32768]{2,1,0:T(2,128)(2,1)}), bf16[2,2,32768]{2,1,0:T(2,128)(2,1)S(1)}, u32[]{:S(2)}, u32[]{:S(2)}) async-start(bf16[2,2,32768]{2,1,0:T(2,128)(2,1)} %reshape.422), calls=%async_computation | async-start | bytes 524288 | tf_op jit(solution)/shard_map/all_to_all | solution.py:91
  89.2 5.5 %all-to-all-done = bf16[2,2,32768]{2,1,0:T(2,128)(2,1)S(1)} async-done(((bf16[2,2,32768]{2,1,0:T(2,128)(2,1)}), bf16[2,2,32768]{2,1,0:T(2,128)(2,1)S(1)}, u32[]{:S(2)}, u32[]{:S(2)}) %all-to-all-start) | async-done | bytes 262176 | tf_op jit(solution)/shard_map/all_to_all | solution.py:91
  94.7 3.4 %all-to-all-start.1 = ((bf16[2,2,32768]{2,1,0:T(2,128)(2,1)}), bf16[2,2,32768]{2,1,0:T(2,128)(2,1)S(1)}, u32[]{:S(2)}, u32[]{:S(2)}) async-start(bf16[2,2,32768]{2,1,0:T(2,128)(2,1)} %reshape.424), calls=%async_computation.1 | async-start | bytes 524288 | tf_op jit(solution)/shard_map/all_to_all | solution.py:92
  98.6 4.7 %all-to-all-done.1 = bf16[2,2,32768]{2,1,0:T(2,128)(2,1)S(1)} async-done(((bf16[2,2,32768]{2,1,0:T(2,128)(2,1)}), bf16[2,2,32768]{2,1,0:T(2,128)(2,1)S(1)}, u32[]{:S(2)}, u32[]{:S(2)}) %all-to-all-start.1) | async-done | bytes 262176 | tf_op jit(solution)/shard_map/all_to_all | solution.py:92
  103.3 3.6 %all-to-all-start.2 = ((bf16[2,2,32768]{2,1,0:T(2,128)(2,1)}), bf16[2,2,32768]{2,1,0:T(2,128)(2,1)S(1)}, u32[]{:S(2)}, u32[]{:S(2)}) async-start(bf16[2,2,32768]{2,1,0:T(2,128)(2,1)} %reshape.426), calls=%async_computation.2 | async-start | bytes 524288 | tf_op jit(solution)/shard_map/all_to_all | solution.py:93
  107.3 4.6 %all-to-all-done.2 = bf16[2,2,32768]{2,1,0:T(2,128)(2,1)S(1)} async-done(((bf16[2,2,32768]{2,1,0:T(2,128)(2,1)}), bf16[2,2,32768]{2,1,0:T(2,128)(2,1)S(1)}, u32[]{:S(2)}, u32[]{:S(2)}) %all-to-all-start.2) | async-done | bytes 262176 | tf_op jit(solution)/shard_map/all_to_all | solution.py:93
  116.7 2.3 %fusion.6 = f32[1,32,16,2,128]{4,2,3,1,0:T(8,128)S(1)} fusion(bf16[32,128,128]{1,2,0:T(8,128)(2,1)} %get-tuple-element.15, bf16[32,128,128]{1,2,0:T(8,128)(2,1)} %get-tuple-element.14, bf16[1,32,16,2,128]{4,2,1,3,0:T(8,128)(2,1)S(1)} %bitcast.196, bf16[1,32,16,2,128]{4,2,1,3,0:T(8,128)(2,1)S(1)} %bitcast.170), kind=kOutput, calls=%fused_computation.9 | convolution fusion | flops 72351744 | bytes 3145728 | tf_op jit(solution)/shard_map/wgcbs,gst->wgcbt/dot_general | solution.py:62
  122.9 2.3 %fusion.16 = (bf16[1,512,256]{1,2,0:T(8,128)(2,1)}, bf16[1,512,256]{1,2,0:T(8,128)(2,1)S(1)}, bf16[1,512,256]{1,2,0:T(8,128)(2,1)}, bf16[1,512,256]{1,2,0:T(8,128)(2,1)S(1)}) fusion(f32[1,512,2,128]{1,3,2,0:T(8,128)} %copy.60, f32[1,512,256]{1,2,0:T(8,128)S(1)} %copy.74, f32[512]{0:T(512)S(1)} %dynamic_slice.7, f32[1,512,2,128]{1,3,2,0:T(8,128)S(1)} %copy.50, ...), kind=kLoop, calls=%fused_computation.30 | loop fusion | flops 1835008 | bytes 4196352 | tf_op jit(solution)/shard_map/convert_element_type | solution.py:69
  126.0 2.2 %reduce.7 = bf16[256,512]{1,0:T(8,128)(2,1)S(1)} reduce(bf16[256,1,512]{2,1,0:T(2,128)(2,1)S(1)} %bitcast.184, bf16[]{:T(256)} %broadcast.146), dimensions={1}, to_apply=%bitcast.148.reduce_sub_computation | reduce | bytes 524290
  129.1 3.4 %all-to-all-start.6 = ((bf16[2,2,32768]{2,1,0:T(2,128)(2,1)}), bf16[2,2,32768]{2,1,0:T(2,128)(2,1)S(1)}, u32[]{:S(2)}, u32[]{:S(2)}) async-start(bf16[2,2,32768]{2,1,0:T(2,128)(2,1)} %reshape.434), calls=%async_computation.6 | async-start | bytes 524288 | tf_op jit(solution)/shard_map/all_to_all | solution.py:107
  132.6 2.7 %fusion.8 = f32[32,128,256,1]{2,1,0,3:T(8,128)} fusion(bf16[32,16,2,128]{3,1,0,2:T(8,128)(2,1)S(1)} %bitcast.171, bf16[1,32,16,2,128]{4,2,1,3,0:T(8,128)(2,1)S(1)} %bitcast.167, bf16[1,32,16,2,128]{4,2,1,3,0:T(8,128)(2,1)S(1)} %bitcast.191), kind=kOutput, calls=%fused_computation.17 | convolution fusion | flops 68157440 | bytes 4980736 | tf_op jit(solution)/shard_map/wgcbt,wgcbs->gts/dot_general | solution.py:71
  135.7 2.2 %reduce.8 = bf16[256,512]{1,0:T(8,128)(2,1)S(1)} reduce(bf16[256,1,512]{2,1,0:T(2,128)(2,1)S(1)} %bitcast.185, bf16[]{:T(256)} %broadcast.146), dimensions={1}, to_apply=%bitcast.147.reduce_sub_computation | reduce | bytes 524290
  139.2 2.2 %reduce.5 = bf16[256,512]{1,0:T(8,128)(2,1)S(1)} reduce(bf16[256,1,512]{2,1,0:T(2,128)(2,1)S(1)} %bitcast.186, bf16[]{:T(256)} %broadcast.146), dimensions={1}, to_apply=%bitcast.150.reduce_sub_computation | reduce | bytes 524290
  142.7 2.2 %reduce.6 = bf16[256,512]{1,0:T(8,128)(2,1)S(1)} reduce(bf16[256,1,512]{2,1,0:T(2,128)(2,1)S(1)} %bitcast.181, bf16[]{:T(256)} %broadcast.146), dimensions={1}, to_apply=%bitcast.149.reduce_sub_computation | reduce | bytes 524290
  145.8 4.6 %copy.93 = f32[4,8,128,256]{3,1,2,0:T(8,128)S(1)} copy(f32[4,8,128,256]{3,2,1,0:T(8,128)} %bitcast.154) | data formatting | bytes 8388608
  150.4 2.3 %pad.6 = f32[32,32896]{1,0:T(8,128)} pad(f32[32,32768]{1,0:T(8,128)S(1)} %bitcast.155, f32[]{:T(128)} %constant.40.clone.1), padding=0_0x0_128 | pad | bytes 8404996 | tf_op jit(solution)/shard_map/jit(_pad)/pad | solution.py:26
  152.8 8.0 %reshape.397 = f32[32,128,257]{2,1,0:T(8,128)} reshape(f32[32,32896]{1,0:T(8,128)} %pad.6) | data formatting | bytes 8421376 | tf_op jit(solution)/shard_map/reshape | solution.py:27
  160.7 3.3 %reduce_sum.18 = f32[32,257]{1,0:T(8,128)S(1)} reduce(f32[32,128,257]{2,1,0:T(8,128)} %reshape.397, f32[]{:T(128)} %constant.40.clone.1), dimensions={1}, to_apply=%region_0.1 | reduce | flops 1044448 | bytes 4243588 | tf_op jit(solution)/shard_map/reduce_sum | solution.py:28
  164.2 3.4 %all-to-all-start.7 = ((bf16[2,2,32768]{2,1,0:T(2,128)(2,1)}), bf16[2,2,32768]{2,1,0:T(2,128)(2,1)S(1)}, u32[]{:S(2)}, u32[]{:S(2)}) async-start(bf16[2,2,32768]{2,1,0:T(2,128)(2,1)} %reshape.436), calls=%async_computation.7 | async-start | bytes 524288 | tf_op jit(solution)/shard_map/all_to_all | solution.py:108
  167.8 19.4 %all-reduce.3 = (f32[32,128]{1,0:T(8,128)S(1)}, f32[512]{0:T(512)S(1)}) all-reduce(f32[32,128]{1,0:T(8,128)S(1)} %rev.3, f32[512]{0:T(512)S(1)} %multiply_reduce_fusion), channel_id=1, replica_groups=mesh['ctx'=2,'dp'=4,'tp'=4] {'dp'}, use_global_device_ids=true, to_apply=%region_1.2 | all-reduce | flops 4608 | bytes 36864 | tf_op jit(solution)/shard_map/psum | solution.py:110
  187.2 4.3 %all-gather = f32[2,1,512]{2,1,0:T(1,128)S(1)} all-gather(f32[1,1,512]{2,1,0:T(1,128)S(1)} %bitcast.202), channel_id=1, replica_groups=mesh['ctx'=2,'dp'=4,'tp'=4] {'ctx'}, dimensions={0}, use_global_device_ids=true | all-gather | bytes 6144 | tf_op jit(solution)/shard_map/all_gather | solution.py:113
  191.6 4.4 %all_gather.6 = f32[64,128]{1,0:T(8,128)S(1)} all-gather(f32[32,128]{1,0:T(8,128)S(1)} %get-tuple-element.6), channel_id=1, replica_groups=mesh['ctx'=2,'dp'=4,'tp'=4] {'ctx'}, dimensions={0}, use_global_device_ids=true | all-gather | bytes 49152 | tf_op jit(solution)/shard_map/all_gather | solution.py:112
  196.0 3.4 %all-to-all-start.3 = ((bf16[2,2,32768]{2,1,0:T(2,128)(2,1)}), bf16[2,2,32768]{2,1,0:T(2,128)(2,1)S(1)}, u32[]{:S(2)}, u32[]{:S(2)}) async-start(bf16[2,2,32768]{2,1,0:T(2,128)(2,1)} %reshape.428), calls=%async_computation.3 | async-start | bytes 524288 | tf_op jit(solution)/shard_map/all_to_all | solution.py:105
  200.0 4.6 %all-to-all-done.3 = bf16[2,2,32768]{2,1,0:T(2,128)(2,1)S(1)} async-done(((bf16[2,2,32768]{2,1,0:T(2,128)(2,1)}), bf16[2,2,32768]{2,1,0:T(2,128)(2,1)S(1)}, u32[]{:S(2)}, u32[]{:S(2)}) %all-to-all-start.3) | async-done | bytes 262176 | tf_op jit(solution)/shard_map/all_to_all | solution.py:105
  204.6 3.4 %all-to-all-start.5 = ((bf16[2,2,32768]{2,1,0:T(2,128)(2,1)}), bf16[2,2,32768]{2,1,0:T(2,128)(2,1)S(1)}, u32[]{:S(2)}, u32[]{:S(2)}) async-start(bf16[2,2,32768]{2,1,0:T(2,128)(2,1)} %reshape.432), calls=%async_computation.5 | async-start | bytes 524288 | tf_op jit(solution)/shard_map/all_to_all | solution.py:106
  (85 shorter events, 32.5 us)
Async XLA Ops:
  0.6 10.0 %copy-start = (f32[64,128]{1,0:T(8,128)S(1)}, f32[64,128]{1,0:T(8,128)}, u32[]{:S(2)}) copy-start(f32[64,128]{1,0:T(8,128)} %param.12) | copy-start | bytes 98308
  6.3 79.1 %all-to-all-start.4 = ((bf16[2,2,32768]{2,1,0:T(2,128)(2,1)}), bf16[2,2,32768]{2,1,0:T(2,128)(2,1)S(1)}, u32[]{:S(2)}, u32[]{:S(2)}) async-start(bf16[2,2,32768]{2,1,0:T(2,128)(2,1)} %reshape.430), calls=%async_computation.4 | async-start | bytes 524288 | tf_op jit(solution)/shard_map/all_to_all | solution.py:94
  72.2 3.0 %copy-start.3 = (bf16[1,1024,128]{2,1,0:T(8,128)(2,1)S(1)}, bf16[1,1024,128]{2,1,0:T(8,128)(2,1)}, u32[]{:S(2)}) copy-start(bf16[1,1024,128]{2,1,0:T(8,128)(2,1)} %param.7) | copy-start | bytes 786436
  72.2 6.3 %copy-start.4 = (bf16[1,1024,128]{2,1,0:T(8,128)(2,1)S(1)}, bf16[1,1024,128]{2,1,0:T(8,128)(2,1)}, u32[]{:S(2)}) copy-start(bf16[1,1024,128]{2,1,0:T(8,128)(2,1)} %param.8) | copy-start | bytes 786436
  73.7 8.2 %copy-start.5 = (bf16[1,1024,128]{2,1,0:T(8,128)(2,1)S(1)}, bf16[1,1024,128]{2,1,0:T(8,128)(2,1)}, u32[]{:S(2)}) copy-start(bf16[1,1024,128]{2,1,0:T(8,128)(2,1)} %param.9) | copy-start | bytes 786436
  73.7 11.6 %copy-start.6 = (f32[1024]{0:T(1024)S(1)}, f32[1024]{0:T(1024)}, u32[]{:S(2)}) copy-start(f32[1024]{0:T(1024)} %param.13) | copy-start | bytes 12292
  85.4 9.3 %all-to-all-start = ((bf16[2,2,32768]{2,1,0:T(2,128)(2,1)}), bf16[2,2,32768]{2,1,0:T(2,128)(2,1)S(1)}, u32[]{:S(2)}, u32[]{:S(2)}) async-start(bf16[2,2,32768]{2,1,0:T(2,128)(2,1)} %reshape.422), calls=%async_computation | async-start | bytes 524288 | tf_op jit(solution)/shard_map/all_to_all | solution.py:91
  94.7 8.6 %all-to-all-start.1 = ((bf16[2,2,32768]{2,1,0:T(2,128)(2,1)}), bf16[2,2,32768]{2,1,0:T(2,128)(2,1)S(1)}, u32[]{:S(2)}, u32[]{:S(2)}) async-start(bf16[2,2,32768]{2,1,0:T(2,128)(2,1)} %reshape.424), calls=%async_computation.1 | async-start | bytes 524288 | tf_op jit(solution)/shard_map/all_to_all | solution.py:92
  103.3 8.6 %all-to-all-start.2 = ((bf16[2,2,32768]{2,1,0:T(2,128)(2,1)}), bf16[2,2,32768]{2,1,0:T(2,128)(2,1)S(1)}, u32[]{:S(2)}, u32[]{:S(2)}) async-start(bf16[2,2,32768]{2,1,0:T(2,128)(2,1)} %reshape.426), calls=%async_computation.2 | async-start | bytes 524288 | tf_op jit(solution)/shard_map/all_to_all | solution.py:93
  125.6 9.7 %copy-start.2 = (bf16[1,512,256]{1,2,0:T(8,128)(2,1)S(1)}, bf16[1,512,256]{1,2,0:T(8,128)(2,1)}, u32[]{:S(2)}) copy-start(bf16[1,512,256]{1,2,0:T(8,128)(2,1)} %get-tuple-element.8) | copy-start | bytes 786436
  129.1 35.1 %all-to-all-start.6 = ((bf16[2,2,32768]{2,1,0:T(2,128)(2,1)}), bf16[2,2,32768]{2,1,0:T(2,128)(2,1)S(1)}, u32[]{:S(2)}, u32[]{:S(2)}) async-start(bf16[2,2,32768]{2,1,0:T(2,128)(2,1)} %reshape.434), calls=%async_computation.6 | async-start | bytes 524288 | tf_op jit(solution)/shard_map/all_to_all | solution.py:107
  132.6 9.8 %copy-start.1 = (bf16[1,512,256]{1,2,0:T(8,128)(2,1)S(1)}, bf16[1,512,256]{1,2,0:T(8,128)(2,1)}, u32[]{:S(2)}) copy-start(bf16[1,512,256]{1,2,0:T(8,128)(2,1)} %get-tuple-element.12) | copy-start | bytes 786436
  164.2 31.8 %all-to-all-start.7 = ((bf16[2,2,32768]{2,1,0:T(2,128)(2,1)}), bf16[2,2,32768]{2,1,0:T(2,128)(2,1)S(1)}, u32[]{:S(2)}, u32[]{:S(2)}) async-start(bf16[2,2,32768]{2,1,0:T(2,128)(2,1)} %reshape.436), calls=%async_computation.7 | async-start | bytes 524288 | tf_op jit(solution)/shard_map/all_to_all | solution.py:108
  196.0 8.6 %all-to-all-start.3 = ((bf16[2,2,32768]{2,1,0:T(2,128)(2,1)}), bf16[2,2,32768]{2,1,0:T(2,128)(2,1)S(1)}, u32[]{:S(2)}, u32[]{:S(2)}) async-start(bf16[2,2,32768]{2,1,0:T(2,128)(2,1)} %reshape.428), calls=%async_computation.3 | async-start | bytes 524288 | tf_op jit(solution)/shard_map/all_to_all | solution.py:105
  204.6 8.6 %all-to-all-start.5 = ((bf16[2,2,32768]{2,1,0:T(2,128)(2,1)}), bf16[2,2,32768]{2,1,0:T(2,128)(2,1)S(1)}, u32[]{:S(2)}, u32[]{:S(2)}) async-start(bf16[2,2,32768]{2,1,0:T(2,128)(2,1)} %reshape.432), calls=%async_computation.5 | async-start | bytes 524288 | tf_op jit(solution)/shard_map/all_to_all | solution.py:106
where the time goes:
time: 215 us; the launch traced here: 214 us
  local copies, waits for them, and re-layouts  97.8 us (45%)
  other arithmetic  31.3 us (15%)
  starting transfers between devices  28.5 us (13%)
  blocking collectives  28.2 us (13%)
  waiting for transfers between devices  20.6 us (10%)
  matrix products  6.98 us (3%)
    gather x2, local copies, waits for them, and re-layouts, tap_matrices(): spread = tap_rows[:, jnp.mod(target - source, tap_len)]  61.4 us
    psum x1, blocking collectives, body(): replica = lax.psum((results[4], results[5]), 'dp')  19.4 us
    unnamed x9, other arithmetic  19.2 us
    unnamed x40, local copies, waits for them, and re-layouts  15.5 us
    reshape x1, local copies, waits for them, and re-layouts, diagonal_sums(): skewed = flattened.reshape(groups, tap_len, double_len + 1)  7.98 us
    all_to_all x1, waiting for transfers between devices, body(): lax.all_to_all(query_act, 'ctx', split_axis=1, concat_axis=2, tiled=True)  5.54 us
    all_to_all x1, waiting for transfers between devices, body(): lax.all_to_all(key_act, 'ctx', split_axis=1, concat_axis=2, tiled=True)  4.75 us
    all_to_all x1, waiting for transfers between devices, body(): lax.all_to_all(value_act, 'ctx', split_axis=1, concat_axis=2, tiled=True)  4.65 us
  transfers between devices with their start and end apart: 8, of which 5 were waited for; matrix products, arithmetic and copies ran while one was open for 52% of the time, Pallas kernels for 0%

commit v1 on v0

--- a/solution.py
+++ b/solution.py
@@ -3,6 +3,15 @@
 import jax.numpy as jnp
 from jax import lax
 from jax.sharding import PartitionSpec as P
+
+
+def get_area(in_array, net_axis):
+    side_arr = lax.axis_size(net_axis)
+    met_up = jnp.split(in_array, side_arr, 1)
+    arr_next = jnp.stack(met_up, 0)
+    taken_in = lax.all_to_all(arr_next, net_axis, 0, 0)
+    base_arr = jnp.concatenate(taken_in, 2)
+    return base_arr
 
 
 def tap_matrices(tap_rows):
@@ -89,7 +98,7 @@
     scaled_grad = out_grad * keep_mask.astype(jnp.bfloat16)[:, None, :]
     moved = (
         lax.all_to_all(query_act, "ctx", split_axis=1, concat_axis=2, tiled=True),
-        lax.all_to_all(key_act, "ctx", split_axis=1, concat_axis=2, tiled=True),
+        get_area(key_act, "ctx"),
         lax.all_to_all(value_act, "ctx", split_axis=1, concat_axis=2, tiled=True),
         lax.all_to_all(scaled_grad, "ctx", split_axis=1, concat_axis=2, tiled=True),
     )

time: 215 us -> 212 us (0.986)
  local copies, waits for them, and re-layouts: 97.8 us -> 94.8 us
    unnamed x9 -> x8, other arithmetic: 19.2 us -> 17 us
    unnamed x40 -> x45, local copies, waits for them, and re-layouts: 15.5 us -> 14 us
  transfers between devices with their start and end apart: 8 -> 8, of which waited for: 5 -> 6; matrix products, arithmetic and copies ran while one was open for 52% -> 53% of each run, Pallas kernels for 0% -> 0%
where the time goes in v1:
time: 212 us; the launch traced here: 210 us
  local copies, waits for them, and re-layouts  94.8 us (45%)
  other arithmetic  29.2 us (14%)
  starting transfers between devices  28.7 us (14%)
  blocking collectives  28.3 us (13%)
  waiting for transfers between devices  21 us (10%)
  matrix products  7.09 us (3%)
    gather x2, local copies, waits for them, and re-layouts, tap_matrices(): spread = tap_rows[:, jnp.mod(target - source, tap_len)]  61.8 us
    psum x1, blocking collectives, body(): replica = lax.psum((results[4], results[5]), 'dp')  19.6 us
    unnamed x8, other arithmetic  17 us
    unnamed x45, local copies, waits for them, and re-layouts  14 us
    reshape x1, local copies, waits for them, and re-layouts, diagonal_sums(): skewed = flattened.reshape(groups, tap_len, double_len + 1)  7.96 us
    all_to_all x1, waiting for transfers between devices, get_area(): taken_in = lax.all_to_all(arr_next, net_axis, 0, 0)  5.34 us
    all_to_all x1, waiting for transfers between devices, body(): lax.all_to_all(results[0], 'ctx', split_axis=2, concat_axis=1, tiled=True)  4.54 us
    all_gather x1, blocking collectives, body(): lax.all_gather(replica[0], 'ctx', axis=0, tiled=True)  4.4 us
  transfers between devices with their start and end apart: 8, of which 6 were waited for; matrix products, arithmetic and copies ran while one was open for 53% of the time, Pallas kernels for 0%

profile of v1, /device:TPU:0, one launch (start us, length us, event | category | flops | bytes accessed | tf_op | source)
XLA Modules:
  0.0 210.4 jit_solution(15993957530461640886)
XLA Ops:
  3.3 2.2 %reduce.3 = bf16[1024,128]{1,0:T(8,128)(2,1)S(1)} reduce(bf16[1024,1,128]{2,1,0:T(2,128)(2,1)S(1)} %fusion.30, bf16[]{:T(256)} %broadcast.146), dimensions={1}, to_apply=%fusion.30.reduce_sub_computation | reduce | bytes 524290
  6.3 4.2 %all-to-all-start.4 = ((bf16[2,2,32768]{2,1,0:T(2,128)(2,1)}), bf16[2,2,32768]{2,1,0:T(2,128)(2,1)S(1)}, u32[]{:S(2)}, u32[]{:S(2)}) async-start(bf16[2,2,32768]{2,1,0:T(2,128)(2,1)} %reshape.426), calls=%async_computation.4 | async-start | bytes 524288 | tf_op jit(solution)/shard_map/all_to_all | solution.py:103
  10.8 57.8 %gather_fusion = bf16[16384,32]{1,0:T(8,128)(2,1)} fusion(bf16[32,128]{0,1:T(8,128)(2,1)S(1)} %copy.95, s32[16384]{0:T(1024)S(1)} %fusion.22), kind=kCustom, calls=%fused_computation | custom fusion | bytes 2162688 | tf_op jit(solution)/shard_map/gather | solution.py:21
  68.6 4.0 %copy.85 = bf16[128,128,32]{1,0,2:T(8,128)(2,1)S(1)} copy(bf16[128,128,32]{2,1,0:T(8,128)(2,1)} %bitcast.160) | data formatting | bytes 2097152 | tf_op jit(solution)/shard_map/gather | solution.py:21
  76.0 2.2 %reduce.2 = bf16[1024,128]{1,0:T(8,128)(2,1)S(1)} reduce(bf16[1024,1,128]{2,1,0:T(2,128)(2,1)S(1)} %bitcast.181, bf16[]{:T(256)} %broadcast.146), dimensions={1}, to_apply=%bitcast.157.reduce_sub_computation | reduce | bytes 524290
  79.4 2.2 %reduce.1 = bf16[1024,128]{1,0:T(8,128)(2,1)S(1)} reduce(bf16[1024,1,128]{2,1,0:T(2,128)(2,1)S(1)} %bitcast.182, bf16[]{:T(256)} %broadcast.146), dimensions={1}, to_apply=%bitcast.156.reduce_sub_computation | reduce | bytes 524290
  83.2 3.5 %all-to-all-start.1 = ((bf16[2,1,512,128]{3,2,1,0:T(8,128)(2,1)}), bf16[2,1,512,128]{3,2,1,0:T(8,128)(2,1)S(1)}, u32[]{:S(2)}, u32[]{:S(2)}) async-start(bf16[2,1,512,128]{3,2,1,0:T(8,128)(2,1)} %pad_maximum_fusion.2), calls=%async_computation.1 | async-start | bytes 524288 | tf_op jit(solution)/shard_map/all_to_all | solution.py:12
  87.2 5.3 %all-to-all-done.1 = bf16[2,1,512,128]{3,2,1,0:T(8,128)(2,1)S(1)} async-done(((bf16[2,1,512,128]{3,2,1,0:T(8,128)(2,1)}), bf16[2,1,512,128]{3,2,1,0:T(8,128)(2,1)S(1)}, u32[]{:S(2)}, u32[]{:S(2)}) %all-to-all-start.1) | async-done | bytes 262176 | tf_op jit(solution)/shard_map/all_to_all | solution.py:12
  92.5 3.4 %all-to-all-start = ((bf16[2,2,32768]{2,1,0:T(2,128)(2,1)}), bf16[2,2,32768]{2,1,0:T(2,128)(2,1)S(1)}, u32[]{:S(2)}, u32[]{:S(2)}) async-start(bf16[2,2,32768]{2,1,0:T(2,128)(2,1)} %reshape.420), calls=%async_computation | async-start | bytes 524288 | tf_op jit(solution)/shard_map/all_to_all | solution.py:100
  97.1 4.1 %all-to-all-done = bf16[2,2,32768]{2,1,0:T(2,128)(2,1)S(1)} async-done(((bf16[2,2,32768]{2,1,0:T(2,128)(2,1)}), bf16[2,2,32768]{2,1,0:T(2,128)(2,1)S(1)}, u32[]{:S(2)}, u32[]{:S(2)}) %all-to-all-start) | async-done | bytes 262176 | tf_op jit(solution)/shard_map/all_to_all | solution.py:100
  101.2 3.6 %all-to-all-start.2 = ((bf16[2,2,32768]{2,1,0:T(2,128)(2,1)}), bf16[2,2,32768]{2,1,0:T(2,128)(2,1)S(1)}, u32[]{:S(2)}, u32[]{:S(2)}) async-start(bf16[2,2,32768]{2,1,0:T(2,128)(2,1)} %reshape.422), calls=%async_computation.2 | async-start | bytes 524288 | tf_op jit(solution)/shard_map/all_to_all | solution.py:102
  105.4 4.3 %all-to-all-done.2 = bf16[2,2,32768]{2,1,0:T(2,128)(2,1)S(1)} async-done(((bf16[2,2,32768]{2,1,0:T(2,128)(2,1)}), bf16[2,2,32768]{2,1,0:T(2,128)(2,1)S(1)}, u32[]{:S(2)}, u32[]{:S(2)}) %all-to-all-start.2) | async-done | bytes 262176 | tf_op jit(solution)/shard_map/all_to_all | solution.py:102
  111.1 2.4 %fusion.6 = f32[1,32,16,2,128]{4,2,3,1,0:T(8,128)S(1)} fusion(bf16[32,128,128]{1,2,0:T(8,128)(2,1)} %get-tuple-element.17, bf16[32,128,128]{1,2,0:T(8,128)(2,1)} %get-tuple-element.16, bf16[1,32,16,2,128]{4,2,1,3,0:T(8,128)(2,1)S(1)} %bitcast.193, bf16[1,32,16,2,128]{4,2,1,3,0:T(8,128)(2,1)S(1)} %bitcast.169), kind=kOutput, calls=%fused_computation.9 | convolution fusion | flops 72351744 | bytes 3145728 | tf_op jit(solution)/shard_map/wgcbs,gst->wgcbt/dot_general | solution.py:71
  114.5 1.9 fusion.7
  117.4 2.1 fusion.16
  120.3 2.2 %reduce.6 = bf16[256,512]{1,0:T(8,128)(2,1)S(1)} reduce(bf16[256,1,512]{2,1,0:T(2,128)(2,1)S(1)} %bitcast.178, bf16[]{:T(256)} %broadcast.146), dimensions={1}, to_apply=%bitcast.153.reduce_sub_computation | reduce | bytes 524290
  123.4 3.4 %all-to-all-start.6 = ((bf16[2,2,32768]{2,1,0:T(2,128)(2,1)}), bf16[2,2,32768]{2,1,0:T(2,128)(2,1)S(1)}, u32[]{:S(2)}, u32[]{:S(2)}) async-start(bf16[2,2,32768]{2,1,0:T(2,128)(2,1)} %reshape.430), calls=%async_computation.6 | async-start | bytes 524288 | tf_op jit(solution)/shard_map/all_to_all | solution.py:116
  127.3 2.2 %reduce.7 = bf16[256,512]{1,0:T(8,128)(2,1)S(1)} reduce(bf16[256,1,512]{2,1,0:T(2,128)(2,1)S(1)} %bitcast.179, bf16[]{:T(256)} %broadcast.146), dimensions={1}, to_apply=%bitcast.152.reduce_sub_computation | reduce | bytes 524290
  132.0 3.7 %all-to-all-start.7 = ((bf16[2,2,32768]{2,1,0:T(2,128)(2,1)}), bf16[2,2,32768]{2,1,0:T(2,128)(2,1)S(1)}, u32[]{:S(2)}, u32[]{:S(2)}) async-start(bf16[2,2,32768]{2,1,0:T(2,128)(2,1)} %reshape.432), calls=%async_computation.7 | async-start | bytes 524288 | tf_op jit(solution)/shard_map/all_to_all | solution.py:117
  135.7 2.7 %fusion.8 = f32[32,128,256,1]{2,1,0,3:T(8,128)} fusion(bf16[32,16,2,128]{3,1,0,2:T(8,128)(2,1)S(1)} %bitcast.170, bf16[1,32,16,2,128]{4,2,1,3,0:T(8,128)(2,1)S(1)} %bitcast.186, bf16[1,32,16,2,128]{4,2,1,3,0:T(8,128)(2,1)S(1)} %bitcast.188), kind=kOutput, calls=%fused_computation.17 | convolution fusion | flops 68157440 | bytes 4980736 | tf_op jit(solution)/shard_map/wgcbt,wgcbs->gts/dot_general | solution.py:80
  138.8 2.2 %reduce.4 = bf16[256,512]{1,0:T(8,128)(2,1)S(1)} reduce(bf16[256,1,512]{2,1,0:T(2,128)(2,1)S(1)} %bitcast.180, bf16[]{:T(256)} %broadcast.146), dimensions={1}, to_apply=%bitcast.155.reduce_sub_computation | reduce | bytes 524290
  142.3 2.2 %reduce.5 = bf16[256,512]{1,0:T(8,128)(2,1)S(1)} reduce(bf16[256,1,512]{2,1,0:T(2,128)(2,1)S(1)} %bitcast.175, bf16[]{:T(256)} %broadcast.146), dimensions={1}, to_apply=%bitcast.154.reduce_sub_computation | reduce | bytes 524290
  145.4 4.6 %copy.96 = f32[4,8,128,256]{3,1,2,0:T(8,128)S(1)} copy(f32[4,8,128,256]{3,2,1,0:T(8,128)} %bitcast.158) | data formatting | bytes 8388608
  150.0 2.3 %pad.6 = f32[32,32896]{1,0:T(8,128)} pad(f32[32,32768]{1,0:T(8,128)S(1)} %bitcast.159, f32[]{:T(128)} %constant.40.clone.1), padding=0_0x0_128 | pad | bytes 8404996 | tf_op jit(solution)/shard_map/jit(_pad)/pad | solution.py:35
  152.3 8.0 %reshape.395 = f32[32,128,257]{2,1,0:T(8,128)} reshape(f32[32,32896]{1,0:T(8,128)} %pad.6) | data formatting | bytes 8421376 | tf_op jit(solution)/shard_map/reshape | solution.py:36
  160.3 3.3 %reduce_sum.18 = f32[32,257]{1,0:T(8,128)S(1)} reduce(f32[32,128,257]{2,1,0:T(8,128)} %reshape.395, f32[]{:T(128)} %constant.40.clone.1), dimensions={1}, to_apply=%region_0.1 | reduce | flops 1044448 | bytes 4243588 | tf_op jit(solution)/shard_map/reduce_sum | solution.py:37
  163.7 19.6 %all-reduce.3 = (f32[32,128]{1,0:T(8,128)S(1)}, f32[512]{0:T(512)S(1)}) all-reduce(f32[32,128]{1,0:T(8,128)S(1)} %rev.3, f32[512]{0:T(512)S(1)} %get-tuple-element.8), channel_id=1, replica_groups=mesh['ctx'=2,'dp'=4,'tp'=4] {'dp'}, use_global_device_ids=true, to_apply=%region_1.2 | all-reduce | flops 4608 | bytes 36864 | tf_op jit(solution)/shard_map/psum | solution.py:119
  183.3 4.3 %all-gather = f32[2,1,512]{2,1,0:T(1,128)S(1)} all-gather(f32[1,1,512]{2,1,0:T(1,128)S(1)} %bitcast.199), channel_id=1, replica_groups=mesh['ctx'=2,'dp'=4,'tp'=4] {'ctx'}, dimensions={0}, use_global_device_ids=true | all-gather | bytes 6144 | tf_op jit(solution)/shard_map/all_gather | solution.py:122
  187.6 4.4 %all_gather.6 = f32[64,128]{1,0:T(8,128)S(1)} all-gather(f32[32,128]{1,0:T(8,128)S(1)} %get-tuple-element.6), channel_id=1, replica_groups=mesh['ctx'=2,'dp'=4,'tp'=4] {'ctx'}, dimensions={0}, use_global_device_ids=true | all-gather | bytes 49152 | tf_op jit(solution)/shard_map/all_gather | solution.py:121
  192.0 3.4 %all-to-all-start.3 = ((bf16[2,2,32768]{2,1,0:T(2,128)(2,1)}), bf16[2,2,32768]{2,1,0:T(2,128)(2,1)S(1)}, u32[]{:S(2)}, u32[]{:S(2)}) async-start(bf16[2,2,32768]{2,1,0:T(2,128)(2,1)} %reshape.424), calls=%async_computation.3 | async-start | bytes 524288 | tf_op jit(solution)/shard_map/all_to_all | solution.py:114
  196.1 4.5 %all-to-all-done.3 = bf16[2,2,32768]{2,1,0:T(2,128)(2,1)S(1)} async-done(((bf16[2,2,32768]{2,1,0:T(2,128)(2,1)}), bf16[2,2,32768]{2,1,0:T(2,128)(2,1)S(1)}, u32[]{:S(2)}, u32[]{:S(2)}) %all-to-all-start.3) | async-done | bytes 262176 | tf_op jit(solution)/shard_map/all_to_all | solution.py:114
  200.7 3.4 %all-to-all-start.5 = ((bf16[2,2,32768]{2,1,0:T(2,128)(2,1)}), bf16[2,2,32768]{2,1,0:T(2,128)(2,1)S(1)}, u32[]{:S(2)}, u32[]{:S(2)}) async-start(bf16[2,2,32768]{2,1,0:T(2,128)(2,1)} %reshape.428), calls=%async_computation.5 | async-start | bytes 524288 | tf_op jit(solution)/shard_map/all_to_all | solution.py:115
  (90 shorter events, 29.3 us)
Async XLA Ops:
  0.6 10.0 %copy-start = (f32[64,128]{1,0:T(8,128)S(1)}, f32[64,128]{1,0:T(8,128)}, u32[]{:S(2)}) copy-start(f32[64,128]{1,0:T(8,128)} %param.12) | copy-start | bytes 98308
  6.3 76.9 %all-to-all-start.4 = ((bf16[2,2,32768]{2,1,0:T(2,128)(2,1)}), bf16[2,2,32768]{2,1,0:T(2,128)(2,1)S(1)}, u32[]{:S(2)}, u32[]{:S(2)}) async-start(bf16[2,2,32768]{2,1,0:T(2,128)(2,1)} %reshape.426), calls=%async_computation.4 | async-start | bytes 524288 | tf_op jit(solution)/shard_map/all_to_all | solution.py:103
  72.6 3.0 %copy-start.9 = (bf16[1,1024,128]{2,1,0:T(8,128)(2,1)S(1)}, bf16[1,1024,128]{2,1,0:T(8,128)(2,1)}, u32[]{:S(2)}) copy-start(bf16[1,1024,128]{2,1,0:T(8,128)(2,1)} %param.8) | copy-start | bytes 786436
  72.6 3.0 %copy-start.7 = (bf16[1,1024,128]{2,1,0:T(8,128)(2,1)S(1)}, bf16[1,1024,128]{2,1,0:T(8,128)(2,1)}, u32[]{:S(2)}) copy-start(bf16[1,1024,128]{2,1,0:T(8,128)(2,1)} %param.7) | copy-start | bytes 786436
  72.6 6.4 %copy-start.8 = (bf16[1,1024,128]{2,1,0:T(8,128)(2,1)S(1)}, bf16[1,1024,128]{2,1,0:T(8,128)(2,1)}, u32[]{:S(2)}) copy-start(bf16[1,1024,128]{2,1,0:T(8,128)(2,1)} %param.9) | copy-start | bytes 786436
  74.1 8.3 %copy-start.10 = (f32[1024]{0:T(1024)S(1)}, f32[1024]{0:T(1024)}, u32[]{:S(2)}) copy-start(f32[1024]{0:T(1024)} %param.13) | copy-start | bytes 12292
  83.2 9.3 %all-to-all-start.1 = ((bf16[2,1,512,128]{3,2,1,0:T(8,128)(2,1)}), bf16[2,1,512,128]{3,2,1,0:T(8,128)(2,1)S(1)}, u32[]{:S(2)}, u32[]{:S(2)}) async-start(bf16[2,1,512,128]{3,2,1,0:T(8,128)(2,1)} %pad_maximum_fusion.2), calls=%async_computation.1 | async-start | bytes 524288 | tf_op jit(solution)/shard_map/all_to_all | solution.py:12
  92.5 8.6 %all-to-all-start = ((bf16[2,2,32768]{2,1,0:T(2,128)(2,1)}), bf16[2,2,32768]{2,1,0:T(2,128)(2,1)S(1)}, u32[]{:S(2)}, u32[]{:S(2)}) async-start(bf16[2,2,32768]{2,1,0:T(2,128)(2,1)} %reshape.420), calls=%async_computation | async-start | bytes 524288 | tf_op jit(solution)/shard_map/all_to_all | solution.py:100
  101.2 8.6 %all-to-all-start.2 = ((bf16[2,2,32768]{2,1,0:T(2,128)(2,1)}), bf16[2,2,32768]{2,1,0:T(2,128)(2,1)S(1)}, u32[]{:S(2)}, u32[]{:S(2)}) async-start(bf16[2,2,32768]{2,1,0:T(2,128)(2,1)} %reshape.422), calls=%async_computation.2 | async-start | bytes 524288 | tf_op jit(solution)/shard_map/all_to_all | solution.py:102
  111.0 3.5 %copy-start.1 = (bf16[1,512,2,128]{3,1,2,0:T(8,128)(2,1)}, bf16[1,512,2,128]{3,1,2,0:T(8,128)(2,1)S(1)}, u32[]{:S(2)}) copy-start(bf16[1,512,2,128]{3,1,2,0:T(8,128)(2,1)S(1)} %get-tuple-element.9) | copy-start | bytes 786436
  111.1 3.4 %copy-start.3 = (bf16[1,512,2,128]{3,1,2,0:T(8,128)(2,1)}, bf16[1,512,2,128]{3,1,2,0:T(8,128)(2,1)S(1)}, u32[]{:S(2)}) copy-start(bf16[1,512,2,128]{3,1,2,0:T(8,128)(2,1)S(1)} %concatenate.29) | copy-start | bytes 786436
  119.5 7.3 %copy-start.6 = (bf16[1,512,256]{1,2,0:T(8,128)(2,1)S(1)}, bf16[1,512,256]{1,2,0:T(8,128)(2,1)}, u32[]{:S(2)}) copy-start(bf16[1,512,256]{1,2,0:T(8,128)(2,1)} %get-tuple-element.10) | copy-start | bytes 786436
  119.5 16.1 %copy-start.2 = (bf16[1,512,2,128]{3,1,2,0:T(8,128)(2,1)S(1)}, bf16[1,512,2,128]{3,1,2,0:T(8,128)(2,1)}, u32[]{:S(2)}) copy-start(bf16[1,512,2,128]{3,1,2,0:T(8,128)(2,1)} %copy-done.1) | copy-start | bytes 786436
  119.5 16.1 %copy-start.4 = (bf16[1,512,2,128]{3,1,2,0:T(8,128)(2,1)S(1)}, bf16[1,512,2,128]{3,1,2,0:T(8,128)(2,1)}, u32[]{:S(2)}) copy-start(bf16[1,512,2,128]{3,1,2,0:T(8,128)(2,1)} %copy-done.3) | copy-start | bytes 786436
  123.4 8.6 %all-to-all-start.6 = ((bf16[2,2,32768]{2,1,0:T(2,128)(2,1)}), bf16[2,2,32768]{2,1,0:T(2,128)(2,1)S(1)}, u32[]{:S(2)}, u32[]{:S(2)}) async-start(bf16[2,2,32768]{2,1,0:T(2,128)(2,1)} %reshape.430), calls=%async_computation.6 | async-start | bytes 524288 | tf_op jit(solution)/shard_map/all_to_all | solution.py:116
  129.5 12.4 %copy-start.5 = (bf16[1,512,256]{1,2,0:T(8,128)(2,1)S(1)}, bf16[1,512,256]{1,2,0:T(8,128)(2,1)}, u32[]{:S(2)}) copy-start(bf16[1,512,256]{1,2,0:T(8,128)(2,1)} %get-tuple-element.14) | copy-start | bytes 786436
  132.0 60.0 %all-to-all-start.7 = ((bf16[2,2,32768]{2,1,0:T(2,128)(2,1)}), bf16[2,2,32768]{2,1,0:T(2,128)(2,1)S(1)}, u32[]{:S(2)}, u32[]{:S(2)}) async-start(bf16[2,2,32768]{2,1,0:T(2,128)(2,1)} %reshape.432), calls=%async_computation.7 | async-start | bytes 524288 | tf_op jit(solution)/shard_map/all_to_all | solution.py:117
  192.0 8.6 %all-to-all-start.3 = ((bf16[2,2,32768]{2,1,0:T(2,128)(2,1)}), bf16[2,2,32768]{2,1,0:T(2,128)(2,1)S(1)}, u32[]{:S(2)}, u32[]{:S(2)}) async-start(bf16[2,2,32768]{2,1,0:T(2,128)(2,1)} %reshape.424), calls=%async_computation.3 | async-start | bytes 524288 | tf_op jit(solution)/shard_map/all_to_all | solution.py:114
  200.7 8.6 %all-to-all-start.5 = ((bf16[2,2,32768]{2,1,0:T(2,128)(2,1)}), bf16[2,2,32768]{2,1,0:T(2,128)(2,1)S(1)}, u32[]{:S(2)}, u32[]{:S(2)}) async-start(bf16[2,2,32768]{2,1,0:T(2,128)(2,1)} %reshape.428), calls=%async_computation.5 | async-start | bytes 524288 | tf_op jit(solution)/shard_map/all_to_all | solution.py:115
